TPU v7x, 32 devices: a whole 2x2x4 slice. The times are simulated.
32 devices in a mesh: scen: 2 (over x), row: 4 (over y, core), col: 4 (over z).
Axes of the slice: x: 2, y: 2, z: 4, core: 2. Of those that a mesh axis runs over, the one named last changes fastest.
Arguments:
- root_matrix: float32 [8192, 8192], P(('scen', 'row'), 'col'), may hold values from -1 to 32, as said below
- inverse_block: bfloat16 [32, 1024, 1024], P(('scen', 'row', 'col')), may hold values from -0.05 to 3, as said below
- link_tiles: bfloat16 [32, 20, 1024, 128], P(('scen', 'row', 'col')), may hold values from -0.1875 to 0.1875
- tile_mask: int32 [32, 64], P(('scen', 'row', 'col')), may hold values from 0 to 1, as said below
- panel_index: int32 [1], replicated, may hold values from 0 to 31
Outputs:
- trailing: float32 [8192, 8192], P(('scen', 'row'), 'col')
- factor: float32 [8192, 128], P(('scen', 'row', 'col'))
Inputs may be any that keep to these rules, and one draw needn't show every extreme that they name: `root_matrix`: Symmetric, with the diagonal between 8 and 32 and every other entry of magnitude under 1. `inverse_block`: each block is symmetric positive definite, its diagonal between 1 and 3. `tile_mask`: each scenario flags between 4 and 20 tiles, at most 4 among each aligned group of 8 tiles (tiles 0 to 7, and so on); some scenario flags exactly 20 tiles, 4 in each of its first groups.
All inputs are finite; a program needn't handle non-finite values.
Results may differ from a plain program's by a relative error of at most 0.00049.
Values may be sent and summed in bfloat16 or wider, within the bound.
A program may use at most 64 MiB of HBM per device.

v0:
```python
import jax
import jax.numpy as jnp
from jax import lax
from jax.sharding import PartitionSpec as P

PANEL = 128


def broadcast(block, axis, source):
    block = jnp.where(lax.axis_index(axis) == source, block, jnp.zeros_like(block))
    return lax.psum(block, axis)


def select_matrix(tile_flags, slot_count):
    slot_order = jnp.cumsum(tile_flags) - 1
    slot_ids = lax.broadcasted_iota(jnp.int32, (slot_count, tile_flags.shape[0]), 0)
    hit = (slot_order[None, :] == slot_ids) & (tile_flags[None, :] == 1)
    return jnp.where(hit, jnp.float32(1.0), jnp.float32(0.0))


def compact_term(inverse, tiles_here, tile_flags, panel_at):
    slot_count, inner_rows, tile_rows = tiles_here.shape
    selector = select_matrix(tile_flags, slot_count)
    per_panel = PANEL // tile_rows
    picked = lax.dynamic_slice_in_dim(selector, panel_at * per_panel, per_panel, 1)
    columns = jnp.einsum(
        "kj,knt->njt", picked.astype(jnp.bfloat16), tiles_here, preferred_element_type=jnp.float32
    )
    columns = columns.reshape(inner_rows, PANEL).astype(jnp.bfloat16)
    weighted = jnp.dot(inverse, columns, preferred_element_type=jnp.float32).astype(jnp.bfloat16)
    product = jnp.einsum("knt,na->kta", tiles_here, weighted, preferred_element_type=jnp.float32)
    return (selector, product)


def dense_term(selector, product, base_cols, base_start):
    spread = jnp.einsum("kr,kta->rta", selector, product, precision=lax.Precision.HIGHEST)
    scenario = spread.reshape(selector.shape[1] * product.shape[1], PANEL)
    own_block = lax.dynamic_slice_in_dim(scenario, base_start, base_cols.shape[0], 0) + base_cols
    return lax.dynamic_update_slice_in_dim(scenario, own_block, base_start, 0)


def lower_rows(diagonal, rows_here, first_row, first_col):
    chol_lower = jnp.linalg.cholesky(diagonal)
    solved = jax.scipy.linalg.solve_triangular(chol_lower, rows_here.T, lower=True).T
    row_ids = first_row + lax.broadcasted_iota(jnp.int32, (rows_here.shape[0], 1), 0)
    return jnp.where(row_ids >= first_col, solved, 0.0)


def trailing_rows(factor_part, first_row, first_col):
    rounded = factor_part.astype(jnp.bfloat16)
    row_ids = first_row + lax.broadcasted_iota(jnp.int32, (factor_part.shape[0], 1), 0)
    return jnp.where(row_ids >= first_col + PANEL, rounded, jnp.zeros_like(rounded))


def local(root_matrix, inverse_block, link_tiles, tile_mask, panel_index):
    panel_at = panel_index[0]
    tile_flags = tile_mask[0]
    selector, product = compact_term(inverse_block[0], link_tiles[0], tile_flags, panel_at)
    tile_count = selector.shape[1]
    tile_rows = product.shape[1]
    total_rows = tile_count * tile_rows
    row_block, col_block = root_matrix.shape
    scen_at = lax.axis_index("scen")
    row_at = lax.axis_index("row")
    col_at = lax.axis_index("col")
    row_count = lax.axis_size("row")
    col_count = lax.axis_size("col")
    scen_count = lax.axis_size("scen")
    block_at = scen_at * row_count + row_at
    first_col = panel_at * PANEL
    owner_col = first_col // col_block
    base_cols = lax.dynamic_slice_in_dim(root_matrix, first_col - owner_col * col_block, PANEL, 1)
    base_cols = jnp.where(col_at == owner_col, base_cols, 0.0)
    piece_rows = row_block // col_count
    scenario = dense_term(selector, product, base_cols, block_at * row_block)
    slab_rows = total_rows // scen_count
    slab_sum = lax.psum_scatter(scenario, "scen", scatter_dimension=0, tiled=True)
    slab_sum = lax.psum(slab_sum, ("row", "col"))
    owner_slab = first_col // slab_rows
    diag_part = lax.dynamic_slice_in_dim(slab_sum, first_col - owner_slab * slab_rows, PANEL, 0)
    diagonal = broadcast(diag_part, "scen", owner_slab)
    slab_first = scen_at * slab_rows
    slab_factor = lower_rows(diagonal, slab_sum, slab_first, first_col)
    factor_rows = lax.dynamic_slice_in_dim(
        slab_factor, (row_at * col_count + col_at) * piece_rows, piece_rows, 0
    )
    ending = trailing_rows(slab_factor, slab_first, first_col)
    all_factor = lax.all_gather(ending, "scen", axis=0, tiled=True)
    own_rows = lax.dynamic_slice_in_dim(all_factor, block_at * row_block, row_block, 0)
    own_cols = lax.dynamic_slice_in_dim(all_factor, col_at * col_block, col_block, 0)
    update = lax.dot_general(
        own_rows, own_cols, (((1,), (1,)), ((), ())), preferred_element_type=jnp.float32
    )
    return (root_matrix - update, factor_rows)


def solution(mesh):
    in_specs = (
        P(("scen", "row"), "col"),
        P(("scen", "row", "col"), None, None),
        P(("scen", "row", "col"), None, None, None),
        P(("scen", "row", "col"), None),
        P(),
    )
    out_specs = (P(("scen", "row"), "col"), P(("scen", "row", "col"), None))
    return jax.shard_map(local, mesh=mesh, in_specs=in_specs, out_specs=out_specs, check_vma=False)
```

profile of v0, /device:TPU:0, one launch (start us, length us, event | category | flops | bytes accessed | tf_op | source)
XLA Modules:
  0.0 295.9 jit_solution(16068640463012025839)
XLA Ops:
  8.1 0.7 compare_bitcast_fusion
  8.7 0.7 copy.11
  9.6 0.1 add_reduce_fusion
  9.8 7.5 %fusion = f32[1,1024,128]{2,0,1:T(1,128)} fusion(bf16[20,1024,128]{2,1,0:T(8,128)(2,1)} %bitcast.50, bf16[20,64]{0,1:T(8,128)(2,1)S(1)} %fusion.24, s32[]{:T(128)S(6)} %select_n.61), kind=kOutput, calls=%fused_computation | convolution fusion | flops 5242880 | bytes 5767684 | tf_op jit(solution)/shard_map/kj,knt->njt/dot_general | solution.py:26
  17.3 4.2 %fusion.13 = f32[128,20,128]{2,0,1:T(8,128)S(1)} fusion(bf16[1,1024,1024]{2,1,0:T(8,128)(2,1)S(1)} %copy-done, f32[1024,128]{1,0:T(8,128)} %bitcast.52, bf16[1,20,1024,128]{3,2,1,0:T(8,128)(2,1)} %param.7), kind=kOutput, calls=%fused_computation.11 | convolution fusion | flops 939786240 | bytes 9175040 | tf_op jit(solution)/shard_map/knt,na->kta/dot_general | solution.py:31
  21.4 1.6 copy.17
  23.1 4.9 %fusion.4 = f32[64,128,128]{2,0,1:T(8,128)S(1)} fusion(f32[128,20,128]{0,1,2:T(8,128)} %copy.17, s32[64]{0:T(128)S(1)} %add_reduce_fusion, pred[64]{0:T(512)(128)(4,1)S(1)} %compare_bitcast_fusion), kind=kOutput, calls=%fused_computation.6 | convolution fusion | flops 251662080 | bytes 5505344 | tf_op jit(solution)/shard_map/kr,kta->rta/dot_general | solution.py:36
  27.9 4.4 %copy.13 = f32[64,128,128]{2,1,0:T(8,128)} copy(f32[64,128,128]{2,0,1:T(8,128)S(1)} %fusion.4) | data formatting | bytes 8388608 | tf_op jit(solution)/shard_map/kr,kta->rta/dot_general | solution.py:36
  32.4 2.0 add_dynamic-update-slice_fusion
  34.5 57.1 %reduce-scatter.2.cloned.1.call-done = f32[4096,128]{1,0:T(8,128)} async-done(((f32[8192,128]{1,0:T(8,128)}), f32[4096,128]{1,0:T(8,128)}) %reduce-scatter.2.cloned.1.call-update) | async-done | bytes 2097168 | tf_op jit(solution)/shard_map/reduce_scatter | solution.py:77
  91.7 101.6 %all-reduce.3.cloned.1.call-done = f32[4096,128]{1,0:T(8,128)} async-done(((f32[4096,128]{1,0:T(8,128)}), f32[4096,128]{1,0:T(8,128)}) %all-reduce.3.cloned.1.call-update) | async-done | bytes 2097168 | tf_op jit(solution)/shard_map/psum | solution.py:78
  193.4 1.5 dynamic-slice_select_fusion
  194.9 0.2 all-gather.2.cloned.1.call-start
  195.1 21.1 %all-reduce.5.cloned.1.call-done = f32[128,128]{1,0:T(8,128)} async-done(((f32[128,128]{1,0:T(8,128)}), f32[128,128]{1,0:T(8,128)}) %all-reduce.5.cloned.1.call-update) | async-done | bytes 65552 | tf_op jit(solution)/shard_map/psum | solution.py:11
  216.3 0.9 copy.14
  217.2 0.9 fusion.21
  218.0 11.7 %cholesky.15 = f32[128,128]{1,0:T(8,128)S(1)} custom-call(f32[128,128]{1,0:T(8,128)S(1)} %fusion.21), custom_call_target="Cholesky" | custom-call | tf_op jit(solution)/shard_map/jit(cholesky)/cholesky | solution.py:43
  229.8 0.6 compare_reduce_fusion
  230.4 0.7 fusion.19
  231.1 9.8 %custom-call.7 = f32[1,128,128]{1,2,0:T(8,128)S(1)} custom-call(f32[1,128,128]{2,1,0:T(8,128)S(1)} %fusion.19), custom_call_target="InvertDiagBlocksLowerTriangular" | custom-call | tf_op jit(solution)/shard_map/jit(_solve_triangular)/triangular_solve | solution.py:44
  240.9 6.8 %convert_select_fusion = (bf16[4096,128]{1,0:T(8,128)(2,1)}, f32[4096,128]{1,0:T(8,128)}) fusion(pred[4096]{0:T(1024)(128)(4,1)S(1)} %fusion.26, f32[4096,128]{1,0:T(8,128)} %all-reduce.3.cloned.1.call-done, f32[1,128,128]{1,2,0:T(8,128)S(1)} %custom-call.7, pred[4096]{0:T(1024)(128)(4,1)S(1)} %fusion.25), kind=kOutput, calls=%fused_computation.10 | convolution fusion | flops 806879232 | bytes 5316608 | tf_op jit(solution)/shard_map/jit(_solve_triangular)/triangular_solve | solution.py:44
  247.8 1.6 constant_dynamic-slice_fusion
  249.3 31.7 %all-gather.2.cloned.1.call-done = bf16[8192,128]{1,0:T(8,128)(2,1)} async-done(((bf16[4096,128]{1,0:T(8,128)(2,1)}), bf16[8192,128]{1,0:T(8,128)(2,1)}) %all-gather.2.cloned.1.call-update) | async-done | bytes 2097168 | tf_op jit(solution)/shard_map/all_gather | solution.py:88
  281.0 8.3 %convolution_subtract_fusion = f32[1024,2048]{1,0:T(8,128)} fusion(f32[1024,2048]{1,0:T(8,128)} %param.5, bf16[8192,128]{1,0:T(8,128)(2,1)} %all-gather.2.cloned.1.call-done, s32[]{:T(128)S(6)} %select_n.74, s32[]{:T(128)S(6)} %select_n.62), kind=kOutput, calls=%fused_computation.3 | convolution fusion | flops 538968064 | bytes 17563656 | tf_op jit(solution)/shard_map/dot_general | solution.py:91
  (14 shorter events, 0.4 us)
Async XLA Ops:
  7.2 10.1 %copy-start = (bf16[1,1024,1024]{2,1,0:T(8,128)(2,1)S(1)}, bf16[1,1024,1024]{2,1,0:T(8,128)(2,1)}, u32[]{:S(2)}) copy-start(bf16[1,1024,1024]{2,1,0:T(8,128)(2,1)} %param.6) | copy-start | bytes 6291460
  7.2 84.4 %reduce-scatter.2.cloned.1.call-start = ((), (), s32[]{:S(2)}) async-start(), calls=%async_computation.1 | async-start | bytes 6291456 | tf_op jit(solution)/shard_map/reduce_scatter | solution.py:77
  34.5 158.9 %all-reduce.3.cloned.1.call-start = ((), (), s32[]{:S(2)}) async-start(), calls=%async_computation.2 | async-start | bytes 4194304 | tf_op jit(solution)/shard_map/psum | solution.py:78
  91.6 124.6 %all-reduce.5.cloned.1.call-start = ((), (), s32[]{:S(2)}) async-start(), calls=%async_computation.3 | async-start | bytes 131072 | tf_op jit(solution)/shard_map/psum | solution.py:11
  194.9 86.2 %all-gather.2.cloned.1.call-start = ((), (), s32[]{:S(2)}) async-start(), calls=%async_computation.4 | async-start | bytes 3145728 | tf_op jit(solution)/shard_map/all_gather | solution.py:88
Sparse Core Ops, SparseCore 0:
  34.6 56.9 reduce-scatter.1
  95.6 97.7 all-reduce.2
  196.2 20.0 all-reduce.4
  247.9 33.1 all-gather.1
where the time goes:
time: 296 us
  waiting for transfers between devices  212 us (72%)
  matrix products  31.7 us (11%)
  other arithmetic  28.2 us (10%)
  between operations  14.7 us (5%)
  local copies, waits for them, and re-layouts  9.31 us (3%)
    psum x1, waiting for transfers between devices, local(): slab_sum = lax.psum(slab_sum, ('row', 'col'))  102 us
    reduce_scatter x1, waiting for transfers between devices, local(): lax.psum_scatter(scenario, 'scen', scatter_dimension=0, tiled=True)  57.1 us
    all_gather x1, waiting for transfers between devices, local(): all_factor = lax.all_gather(ending, 'scen', axis=0, tiled=True)  31.7 us
    psum x1, waiting for transfers between devices, broadcast(): return lax.psum(block, axis)  21.1 us
    another operation x3, other arithmetic, lower_rows(): chol_lower = jnp.linalg.cholesky(diagonal)  12.4 us
    another operation x2, other arithmetic, lower_rows(): jax.scipy.linalg.solve_triangular(chol_lower, rows_here.T, lower=True)  10.5 us
    dot_general x1, matrix products, local(): lax.dot_general(own_rows, own_cols, (((1,), (1,)), ((), ())), preferred_e...  8.3 us
    dot_general x1, matrix products, compact_term(): jnp.einsum('kj,knt->njt', picked.astype(jnp.bfloat16), tiles_here, prefer...  7.47 us
  transfers between devices with their start and end apart: 4, of which 4 were waited for; matrix products, arithmetic and copies ran while one was open for 1% of the time, Pallas kernels for 0%

commit v1 on v0

--- a/solution.py
+++ b/solution.py
@@ -75,7 +75,10 @@
     scenario = dense_term(selector, product, base_cols, block_at * row_block)
     slab_rows = total_rows // scen_count
     slab_sum = lax.psum_scatter(scenario, "scen", scatter_dimension=0, tiled=True)
-    slab_sum = lax.psum(slab_sum, ("row", "col"))
+    original = slab_sum
+    for c in ("col", "row"):
+        original = lax.psum(original, axis_name=c)
+    slab_sum = original
     owner_slab = first_col // slab_rows
     diag_part = lax.dynamic_slice_in_dim(slab_sum, first_col - owner_slab * slab_rows, PANEL, 0)
     diagonal = broadcast(diag_part, "scen", owner_slab)

time: 296 us -> 337 us (1.14)
  waiting for transfers between devices: 212 us -> 252 us
    psum x1 -> x2, waiting for transfers between devices: 102 us -> 142 us  [local(): original = lax.psum(original, axis_name=c)]
  transfers between devices with their start and end apart: 4 -> 5, of which waited for: 4 -> 5; matrix products, arithmetic and copies ran while one was open for 1% -> 0% of each run, Pallas kernels for 0% -> 0%
where the time goes in v1:
time: 337 us
  waiting for transfers between devices  252 us (75%)
  matrix products  31.7 us (9%)
  other arithmetic  28.2 us (8%)
  between operations  14.7 us (4%)
  local copies, waits for them, and re-layouts  9.31 us (3%)
    psum x2, waiting for transfers between devices, local(): original = lax.psum(original, axis_name=c)  142 us
    reduce_scatter x1, waiting for transfers between devices, local(): lax.psum_scatter(scenario, 'scen', scatter_dimension=0, tiled=True)  57.1 us
    all_gather x1, waiting for transfers between devices, local(): all_factor = lax.all_gather(ending, 'scen', axis=0, tiled=True)  31.7 us
    psum x1, waiting for transfers between devices, broadcast(): return lax.psum(block, axis)  21.9 us
    another operation x3, other arithmetic, lower_rows(): chol_lower = jnp.linalg.cholesky(diagonal)  12.4 us
    another operation x2, other arithmetic, lower_rows(): jax.scipy.linalg.solve_triangular(chol_lower, rows_here.T, lower=True)  10.5 us
    dot_general x1, matrix products, local(): lax.dot_general(own_rows, own_cols, (((1,), (1,)), ((), ())), preferred_e...  8.3 us
    dot_general x1, matrix products, compact_term(): jnp.einsum('kj,knt->njt', picked.astype(jnp.bfloat16), tiles_here, prefer...  7.47 us
  transfers between devices with their start and end apart: 5, of which 5 were waited for; matrix products, arithmetic and copies ran while one was open for 0% of the time, Pallas kernels for 0%

profile of v1, /device:TPU:0, one launch (start us, length us, event | category | flops | bytes accessed | tf_op | source)
XLA Modules:
  0.0 336.6 jit_solution(2640348039849032946)
XLA Ops:
  8.1 0.7 compare_bitcast_fusion
  8.7 0.7 copy.11
  9.8 7.5 %fusion = f32[1,1024,128]{2,0,1:T(1,128)} fusion(bf16[20,1024,128]{2,1,0:T(8,128)(2,1)} %bitcast.50, bf16[20,64]{0,1:T(8,128)(2,1)S(1)} %fusion.24, s32[]{:T(128)S(6)} %select_n.61), kind=kOutput, calls=%fused_computation | convolution fusion | flops 5242880 | bytes 5767684 | tf_op jit(solution)/shard_map/kj,knt->njt/dot_general | solution.py:26
  17.3 4.2 %fusion.13 = f32[128,20,128]{2,0,1:T(8,128)S(1)} fusion(bf16[1,1024,1024]{2,1,0:T(8,128)(2,1)S(1)} %copy-done, f32[1024,128]{1,0:T(8,128)} %bitcast.52, bf16[1,20,1024,128]{3,2,1,0:T(8,128)(2,1)} %param.7), kind=kOutput, calls=%fused_computation.11 | convolution fusion | flops 939786240 | bytes 9175040 | tf_op jit(solution)/shard_map/knt,na->kta/dot_general | solution.py:31
  21.4 1.6 copy.17
  23.1 4.9 %fusion.4 = f32[64,128,128]{2,0,1:T(8,128)S(1)} fusion(f32[128,20,128]{0,1,2:T(8,128)} %copy.17, s32[64]{0:T(128)S(1)} %add_reduce_fusion, pred[64]{0:T(512)(128)(4,1)S(1)} %compare_bitcast_fusion), kind=kOutput, calls=%fused_computation.6 | convolution fusion | flops 251662080 | bytes 5505344 | tf_op jit(solution)/shard_map/kr,kta->rta/dot_general | solution.py:36
  27.9 4.4 %copy.13 = f32[64,128,128]{2,1,0:T(8,128)} copy(f32[64,128,128]{2,0,1:T(8,128)S(1)} %fusion.4) | data formatting | bytes 8388608 | tf_op jit(solution)/shard_map/kr,kta->rta/dot_general | solution.py:36
  32.4 2.0 add_dynamic-update-slice_fusion
  34.5 57.1 %reduce-scatter.2.cloned.1.call-done = f32[4096,128]{1,0:T(8,128)} async-done(((f32[8192,128]{1,0:T(8,128)}), f32[4096,128]{1,0:T(8,128)}) %reduce-scatter.2.cloned.1.call-update) | async-done | bytes 2097168 | tf_op jit(solution)/shard_map/reduce_scatter | solution.py:77
  91.7 88.9 %all-reduce.4.cloned.1.call-done = f32[4096,128]{1,0:T(8,128)} async-done(((f32[4096,128]{1,0:T(8,128)}), f32[4096,128]{1,0:T(8,128)}) %all-reduce.4.cloned.1.call-update) | async-done | bytes 2097168 | tf_op jit(solution)/shard_map/psum | solution.py:80
  180.8 52.6 %all-reduce.6.cloned.1.call-done = f32[4096,128]{1,0:T(8,128)} async-done(((f32[4096,128]{1,0:T(8,128)}), f32[4096,128]{1,0:T(8,128)}) %all-reduce.6.cloned.1.call-update) | async-done | bytes 2097168 | tf_op jit(solution)/shard_map/psum | solution.py:80
  233.4 1.5 dynamic-slice_select_fusion
  234.9 0.2 all-gather.2.cloned.1.call-start
  235.1 21.9 %all-reduce.8.cloned.1.call-done = f32[128,128]{1,0:T(8,128)} async-done(((f32[128,128]{1,0:T(8,128)}), f32[128,128]{1,0:T(8,128)}) %all-reduce.8.cloned.1.call-update) | async-done | bytes 65552 | tf_op jit(solution)/shard_map/psum | solution.py:11
  257.0 0.9 copy.14
  257.9 0.9 fusion.21
  258.8 11.7 %cholesky.15 = f32[128,128]{1,0:T(8,128)S(1)} custom-call(f32[128,128]{1,0:T(8,128)S(1)} %fusion.21), custom_call_target="Cholesky" | custom-call | tf_op jit(solution)/shard_map/jit(cholesky)/cholesky | solution.py:43
  270.5 0.6 compare_reduce_fusion
  271.2 0.7 fusion.19
  271.9 9.8 %custom-call.7 = f32[1,128,128]{1,2,0:T(8,128)S(1)} custom-call(f32[1,128,128]{2,1,0:T(8,128)S(1)} %fusion.19), custom_call_target="InvertDiagBlocksLowerTriangular" | custom-call | tf_op jit(solution)/shard_map/jit(_solve_triangular)/triangular_solve | solution.py:44
  281.7 6.8 %convert_select_fusion = (bf16[4096,128]{1,0:T(8,128)(2,1)}, f32[4096,128]{1,0:T(8,128)}) fusion(pred[4096]{0:T(1024)(128)(4,1)S(1)} %fusion.26, f32[4096,128]{1,0:T(8,128)} %all-reduce.6.cloned.1.call-done, f32[1,128,128]{1,2,0:T(8,128)S(1)} %custom-call.7, pred[4096]{0:T(1024)(128)(4,1)S(1)} %fusion.25), kind=kOutput, calls=%fused_computation.10 | convolution fusion | flops 806879232 | bytes 5316608 | tf_op jit(solution)/shard_map/jit(_solve_triangular)/triangular_solve | solution.py:44
  288.5 1.6 constant_dynamic-slice_fusion
  290.1 31.7 %all-gather.2.cloned.1.call-done = bf16[8192,128]{1,0:T(8,128)(2,1)} async-done(((bf16[4096,128]{1,0:T(8,128)(2,1)}), bf16[8192,128]{1,0:T(8,128)(2,1)}) %all-gather.2.cloned.1.call-update) | async-done | bytes 2097168 | tf_op jit(solution)/shard_map/all_gather | solution.py:91
  321.8 8.3 %convolution_subtract_fusion = f32[1024,2048]{1,0:T(8,128)} fusion(f32[1024,2048]{1,0:T(8,128)} %param.5, bf16[8192,128]{1,0:T(8,128)(2,1)} %all-gather.2.cloned.1.call-done, s32[]{:T(128)S(6)} %select_n.74, s32[]{:T(128)S(6)} %select_n.62), kind=kOutput, calls=%fused_computation.3 | convolution fusion | flops 538968064 | bytes 17563656 | tf_op jit(solution)/shard_map/dot_general | solution.py:94
  (17 shorter events, 0.6 us)
Async XLA Ops:
  7.2 10.1 %copy-start = (bf16[1,1024,1024]{2,1,0:T(8,128)(2,1)S(1)}, bf16[1,1024,1024]{2,1,0:T(8,128)(2,1)}, u32[]{:S(2)}) copy-start(bf16[1,1024,1024]{2,1,0:T(8,128)(2,1)} %param.6) | copy-start | bytes 6291460
  7.2 84.4 %reduce-scatter.2.cloned.1.call-start = ((), (), s32[]{:S(2)}) async-start(), calls=%async_computation.1 | async-start | bytes 6291456 | tf_op jit(solution)/shard_map/reduce_scatter | solution.py:77
  34.5 146.2 %all-reduce.4.cloned.1.call-start = ((), (), s32[]{:S(2)}) async-start(), calls=%async_computation.2 | async-start | bytes 4194304 | tf_op jit(solution)/shard_map/psum | solution.py:80
  91.6 141.7 %all-reduce.6.cloned.1.call-start = ((), (), s32[]{:S(2)}) async-start(), calls=%async_computation.3 | async-start | bytes 4194304 | tf_op jit(solution)/shard_map/psum | solution.py:80
  180.7 76.3 %all-reduce.8.cloned.1.call-start = ((), (), s32[]{:S(2)}) async-start(), calls=%async_computation.4 | async-start | bytes 131072 | tf_op jit(solution)/shard_map/psum | solution.py:11
  234.9 86.9 %all-gather.2.cloned.1.call-start = ((), (), s32[]{:S(2)}) async-start(), calls=%async_computation.5 | async-start | bytes 3145728 | tf_op jit(solution)/shard_map/all_gather | solution.py:91
Sparse Core Ops, SparseCore 0:
  34.6 56.9 reduce-scatter.1
  94.1 86.4 all-reduce.3
  183.0 50.3 all-reduce.5
  236.1 20.8 all-reduce.7
  288.6 33.1 all-gather.1
